TPU v7x, 512 devices: a whole 4x4x16 slice. The times are simulated.
512 devices in a mesh: rows: 64 (over x, z_lo, core), cols: 8 (over y, z_hi).
Axes of the slice: x: 4, y: 4, z: 16 (z_hi: 2, z_lo: 8; z = z_hi * 8 + z_lo), core: 2. Of those that a mesh axis runs over, the one named last changes fastest.
Arguments:
- features: bfloat16 [786432, 256], P(('rows', 'cols')), may hold values from -6 to 6
- adj_values: bfloat16 [6144, 3, 128, 128], P(('rows', 'cols')), may hold values from -0.3125 to 0.3125
- adj_offset: int32 [6144, 3], P(('rows', 'cols')), may hold values from -2 to 2, as said below
- adj_count: int32 [6144], P(('rows', 'cols')), may hold values from 1 to 3, as said below
- weight: bfloat16 [256, 256], replicated, may hold values from -0.375 to 0.375
- bias_vector: float32 [256], replicated, may hold values from -4 to 4
- cotangent: bfloat16 [786432, 256], P(('rows', 'cols')), may hold values from -6 to 6
Outputs:
- activated: bfloat16 [786432, 256], P(('rows', 'cols'))
- grad_features: bfloat16 [786432, 256], P(('rows', 'cols'))
- grad_weight: float32 [256, 256], replicated
- grad_bias: float32 [256], replicated
Inputs may be any that keep to these rules, and one draw needn't show every extreme that they name: Slot 0 of every row block has offset 0; the offsets of one row block are distinct, and for row block i every i + adj_offset[i, s] lies in 0 to 6143. Row block i uses its slots 0 to adj_count[i] - 1; the values and offsets of its other slots are ignored. In every draw all row blocks of one device, drawn from the seed, use all 3 slots.
All inputs are finite; a program needn't handle non-finite values.
Results may differ from a plain program's by a relative error of at most 0.0075.
Values may be sent and summed in bfloat16 or wider, within the bound.
A program may use at most 64 MiB of HBM per device.

v0:
```python
import math

import jax
import jax.numpy as jnp
from jax import lax
from jax.sharding import PartitionSpec as P

BAND = 2


def shifted(value, axis, steps):
    count = lax.axis_size(axis)
    pairs = [(source, (source + steps) % count) for source in range(count)]
    return lax.ppermute(value, axis, pairs)


def from_behind(value, axis, steps):
    count = lax.axis_size(axis)
    initial, last = (max(0, -steps), min(count, count - steps))
    return lax.ppermute(value, axis, [(source, source + steps) for source in range(initial, last)])


def fetch_lower(rim_piece):
    narrow_step = shifted(rim_piece, "cols", 1)
    wide_step = from_behind(narrow_step, "rows", 1)
    return jnp.where(lax.axis_index("cols") == 0, wide_step, narrow_step)


def fetch_upper(rim_piece):
    narrow_step = shifted(rim_piece, "cols", -1)
    wide_step = from_behind(narrow_step, "rows", -1)
    return jnp.where(lax.axis_index("cols") == lax.axis_size("cols") - 1, wide_step, narrow_step)


def spill_lower(rim_piece):
    narrow_step = shifted(rim_piece, "cols", 1)
    wide_step = from_behind(narrow_step, "rows", 1)
    return jnp.where(lax.axis_index("cols") == 0, wide_step, narrow_step)


def spill_upper(rim_piece):
    narrow_step = shifted(rim_piece, "cols", -1)
    wide_step = from_behind(narrow_step, "rows", -1)
    return jnp.where(lax.axis_index("cols") == lax.axis_size("cols") - 1, wide_step, narrow_step)


def on_device(features, adj_values, adj_offset, adj_count, weight, bias_vector, cotangent):
    blocks = adj_offset.shape[0]
    slot_total = adj_offset.shape[1]
    block_rows = adj_values.shape[2]
    feat_width = features.shape[1]
    band_reach = BAND
    span_blocks = blocks + 2 * band_reach
    rim_rows = band_reach * block_rows
    slot_index = lax.broadcasted_iota(jnp.int32, (blocks, slot_total), 1)
    block_index = lax.broadcasted_iota(jnp.int32, (blocks, slot_total), 0)
    active = slot_index < adj_count[:, None]
    target = block_index + band_reach + adj_offset
    from_below = fetch_lower(features[features.shape[0] - rim_rows :])
    from_above = fetch_upper(features[:rim_rows])
    extended = jnp.concatenate([from_below, features, from_above], 0)
    window = extended.reshape(span_blocks, block_rows, feat_width)
    picked = window[target]
    picked = jnp.where(active[:, :, None, None], picked, jnp.zeros_like(picked))
    summed = jnp.einsum("bsac,bscf->baf", adj_values, picked, preferred_element_type=jnp.float32)
    aggregated = summed.reshape(-1, feat_width).astype(jnp.bfloat16)
    preact = jnp.dot(aggregated, weight, preferred_element_type=jnp.float32) + bias_vector
    activated = jax.nn.silu(preact).astype(jnp.bfloat16)
    sigmoid_pre = jax.nn.sigmoid(preact)
    grad_pre = (
        cotangent.astype(jnp.float32) * sigmoid_pre * (1.0 + preact * (1.0 - sigmoid_pre))
    ).astype(jnp.bfloat16)
    partial_weight = lax.dot_general(
        aggregated, grad_pre, (((0,), (0,)), ((), ())), preferred_element_type=jnp.float32
    )
    partial_bias = jnp.sum(grad_pre.astype(jnp.float32), axis=0)
    total_weight, total_bias = lax.psum((partial_weight, partial_bias), ("rows", "cols"))
    nodes_total = features.shape[0] * lax.axis_size("rows") * lax.axis_size("cols")
    norm_scale = 1.0 / math.sqrt(nodes_total)
    grad_weight = total_weight * norm_scale
    grad_bias = total_bias * norm_scale
    upstream = lax.dot_general(
        grad_pre, weight, (((1,), (1,)), ((), ())), preferred_element_type=jnp.float32
    ).astype(jnp.bfloat16)
    slot_terms = jnp.einsum(
        "bsac,baf->bscf",
        adj_values,
        upstream.reshape(blocks, block_rows, feat_width),
        preferred_element_type=jnp.float32,
    )
    slot_terms = jnp.where(active[:, :, None, None], slot_terms, jnp.zeros_like(slot_terms))
    empty = jnp.zeros((span_blocks, block_rows, feat_width), jnp.float32)
    spread = empty.at[target.reshape(-1)].add(slot_terms.reshape(-1, block_rows, feat_width))
    lower_part = spread[:band_reach]
    middle = spread[band_reach : band_reach + blocks]
    upper_part = spread[band_reach + blocks :]
    from_above_dev = spill_upper(lower_part)
    from_below_dev = spill_lower(upper_part)
    combined = middle.at[:band_reach].add(from_below_dev)
    combined = combined.at[blocks - band_reach :].add(from_above_dev)
    grad_features = combined.reshape(-1, feat_width).astype(jnp.bfloat16)
    return (activated, grad_features, grad_weight, grad_bias)


def solution(mesh):
    return jax.shard_map(
        on_device,
        mesh=mesh,
        in_specs=(
            P(("rows", "cols"), None),
            P(("rows", "cols"), None, None, None),
            P(("rows", "cols"), None),
            P(("rows", "cols")),
            P(),
            P(),
            P(("rows", "cols"), None),
        ),
        out_specs=(P(("rows", "cols"), None), P(("rows", "cols"), None), P(), P()),
        check_vma=False,
    )
```

profile of v0, /device:TPU:1, one launch (start us, length us, event | category | flops | bytes accessed | tf_op | source)
XLA Modules:
  0.0 578.4 jit_solution(4762388384572714263)
XLA Ops:
  7.2 1.1 fusion.11
  8.4 16.3 %collective-permute-start = (bf16[256,256]{1,0:T(8,128)(2,1)S(1)}, bf16[256,256]{1,0:T(8,128)(2,1)S(1)}, u32[]{:S(2)}, u32[]{:S(2)}) collective-permute-start(bf16[256,256]{1,0:T(8,128)(2,1)S(1)} %get-tuple-element.35), channel_id=1, source_target_pairs={{0,1},{1,2},{2,3},{3,4},{4,5},{5,6},{6,7},{7,0},{8,9},{9,10},{10,1... | collective-permute-start | bytes 393224 | tf_op jit(solution)/shard_map/ppermute | solution.py:14
  24.6 4.4 collective-permute-start.2
  29.0 0.7 compare_select_fusion
  29.9 0.7 iota_compare_fusion
  30.6 12.2 %collective-permute-start.1 = (bf16[256,256]{1,0:T(8,128)(2,1)S(1)}, bf16[256,256]{1,0:T(8,128)(2,1)S(1)}, u32[]{:S(2)}, u32[]{:S(2)}) collective-permute-start(bf16[256,256]{1,0:T(8,128)(2,1)S(1)} %collective-permute-done), channel_id=1, source_target_pairs={{0,8},{8,16},{16,24},{24,32},{32,40},{40,48},{48,56},{56,64},{64,7... | collective-permute-start | bytes 393224 | tf_op jit(solution)/shard_map/ppermute | solution.py:20
  43.0 6.0 %collective-permute-done.2 = bf16[256,256]{1,0:T(8,128)(2,1)S(1)} collective-permute-done((bf16[256,256]{1,0:T(8,128)(2,1)S(1)}, bf16[256,256]{1,0:T(8,128)(2,1)S(1)}, u32[]{:S(2)}, u32[]{:S(2)}) %collective-permute-start.2) | collective-permute-done | bytes 131104 | tf_op jit(solution)/shard_map/ppermute | solution.py:14
  49.0 6.4 %collective-permute-start.3 = (bf16[256,256]{1,0:T(8,128)(2,1)S(1)}, bf16[256,256]{1,0:T(8,128)(2,1)S(1)}, u32[]{:S(2)}, u32[]{:S(2)}) collective-permute-start(bf16[256,256]{1,0:T(8,128)(2,1)S(1)} %collective-permute-done.2), channel_id=1, source_target_pairs={{8,0},{16,8},{24,16},{32,24},{40,32},{48,40},{56,48},{64,56},{72,6... | collective-permute-start | bytes 393224 | tf_op jit(solution)/shard_map/ppermute | solution.py:20
  55.5 0.9 collective-permute-done.3
  56.5 2.3 gather_fusion
  58.8 2.4 bitcast_convert_fusion
  61.3 1.8 convert_reduce_fusion
  63.1 0.9 copy-done.2
  64.0 0.4 convolution_convert_fusion
  64.4 3.1 broadcast_select_fusion
  67.5 6.1 %copy.17 = f32[36,128,256]{2,1,0:T(8,128)} copy(f32[36,128,256]{1,2,0:T(8,128)} %bitcast.28) | data formatting | bytes 9437184 | tf_op jit(solution)/shard_map/reshape | solution.py:93
  73.6 0.2 broadcast_in_dim.36
  73.8 8.8 %scatter_fusion = f32[16,128,256]{2,1,0:T(8,128)S(1)} fusion(f32[16,128,256]{2,1,0:T(8,128)S(1)} %broadcast_in_dim.36, s32[36]{0:T(128)S(1)} %fusion.8, f32[36,128,256]{2,1,0:T(8,128)} %copy.17), kind=kCustom, calls=%fused_computation.1 | custom fusion | flops 1179648 | bytes 14155920 | tf_op jit(solution)/shard_map/scatter-add | solution.py:93
  82.7 0.8 fusion.10
  83.5 10.6 %collective-permute-start.4 = (f32[2,128,256]{2,1,0:T(8,128)}, f32[2,128,256]{2,1,0:T(8,128)}, u32[]{:S(2)}, u32[]{:S(2)}) collective-permute-start(f32[2,128,256]{2,1,0:T(8,128)} %get-tuple-element.33), channel_id=1, source_target_pairs={{0,1},{1,2},{2,3},{3,4},{4,5},{5,6},{6,7},{7,0},{8,9},{9,10},{10,1... | collective-permute-start | bytes 786440 | tf_op jit(solution)/shard_map/ppermute | solution.py:14
  94.2 5.5 collective-permute-start.6
  99.6 2.5 fusion.12
  102.1 110.8 %psum.15 = f32[256]{0:T(256)S(1)} all-reduce(f32[256]{0:T(256)S(1)} %get-tuple-element.28), channel_id=1, replica_groups=mesh['rows'=64,'cols'=8] {'rows','cols'}, use_global_device_ids=true, to_apply=%region_3.4 | all-reduce | flops 256 | bytes 2048 | tf_op jit(solution)/shard_map/psum | solution.py:77
  213.0 1.9 collective-permute-start.5
  214.9 0.6 broadcast_multiply_fusion.1
  215.5 1.3 slice.73
  216.8 3.1 collective-permute-start.7
  219.9 344.2 %all-reduce.2.cloned.1.call-done = f32[256,256]{1,0:T(8,128)} async-done(((f32[256,256]{1,0:T(8,128)}), f32[256,256]{1,0:T(8,128)}) %all-reduce.2.cloned.1.call-update) | async-done | bytes 262160 | tf_op jit(solution)/shard_map/psum | solution.py:77
  564.1 1.7 broadcast_multiply_fusion
  565.8 1.7 fusion.7
  567.5 1.7 fusion.6
  569.2 2.4 convert_element_type.37
  (31 shorter events, 0.6 us)
Async XLA Ops:
  7.2 51.7 %copy-start = (bf16[12,3,128,128]{3,2,1,0:T(8,128)(2,1)S(1)}, bf16[12,3,128,128]{3,2,1,0:T(8,128)(2,1)}, u32[]{:S(2)}) copy-start(bf16[12,3,128,128]{3,2,1,0:T(8,128)(2,1)} %param.12) | copy-start | bytes 3538948
  7.2 49.3 %copy-start.1 = (bf16[1536,256]{1,0:T(8,128)(2,1)S(1)}, bf16[1536,256]{1,0:T(8,128)(2,1)}, u32[]{:S(2)}) copy-start(bf16[1536,256]{1,0:T(8,128)(2,1)} %param.11) | copy-start | bytes 2359300
  7.2 556.9 %all-reduce.2.cloned.1.call-start = ((), (), s32[]{:S(2)}) async-start(), calls=%async_computation | async-start | bytes 524288 | tf_op jit(solution)/shard_map/psum | solution.py:77
  8.4 22.3 %collective-permute-start = (bf16[256,256]{1,0:T(8,128)(2,1)S(1)}, bf16[256,256]{1,0:T(8,128)(2,1)S(1)}, u32[]{:S(2)}, u32[]{:S(2)}) collective-permute-start(bf16[256,256]{1,0:T(8,128)(2,1)S(1)} %get-tuple-element.35), channel_id=1, source_target_pairs={{0,1},{1,2},{2,3},{3,4},{4,5},{5,6},{6,7},{7,0},{8,9},{9,10},{10,1... | collective-permute-start | bytes 393224 | tf_op jit(solution)/shard_map/ppermute | solution.py:14
  24.6 24.4 %collective-permute-start.2 = (bf16[256,256]{1,0:T(8,128)(2,1)S(1)}, bf16[256,256]{1,0:T(8,128)(2,1)S(1)}, u32[]{:S(2)}, u32[]{:S(2)}) collective-permute-start(bf16[256,256]{1,0:T(8,128)(2,1)S(1)} %get-tuple-element.36), channel_id=1, source_target_pairs={{0,7},{1,0},{2,1},{3,2},{4,3},{5,4},{6,5},{7,6},{8,15},{9,8},{10,9... | collective-permute-start | bytes 393224 | tf_op jit(solution)/shard_map/ppermute | solution.py:14
  30.6 24.8 %collective-permute-start.1 = (bf16[256,256]{1,0:T(8,128)(2,1)S(1)}, bf16[256,256]{1,0:T(8,128)(2,1)S(1)}, u32[]{:S(2)}, u32[]{:S(2)}) collective-permute-start(bf16[256,256]{1,0:T(8,128)(2,1)S(1)} %collective-permute-done), channel_id=1, source_target_pairs={{0,8},{8,16},{16,24},{24,32},{32,40},{40,48},{48,56},{56,64},{64,7... | collective-permute-start | bytes 393224 | tf_op jit(solution)/shard_map/ppermute | solution.py:20
  49.0 7.4 %collective-permute-start.3 = (bf16[256,256]{1,0:T(8,128)(2,1)S(1)}, bf16[256,256]{1,0:T(8,128)(2,1)S(1)}, u32[]{:S(2)}, u32[]{:S(2)}) collective-permute-start(bf16[256,256]{1,0:T(8,128)(2,1)S(1)} %collective-permute-done.2), channel_id=1, source_target_pairs={{8,0},{16,8},{24,16},{32,24},{40,32},{48,40},{56,48},{64,56},{72,6... | collective-permute-start | bytes 393224 | tf_op jit(solution)/shard_map/ppermute | solution.py:20
  58.8 2.4 copy-start.3
  58.8 2.4 copy-start.4
  58.8 2.5 copy-start.5
  61.2 1.9 copy-start.6
  63.1 0.9 copy-start.2
  83.5 129.5 %collective-permute-start.4 = (f32[2,128,256]{2,1,0:T(8,128)}, f32[2,128,256]{2,1,0:T(8,128)}, u32[]{:S(2)}, u32[]{:S(2)}) collective-permute-start(f32[2,128,256]{2,1,0:T(8,128)} %get-tuple-element.33), channel_id=1, source_target_pairs={{0,1},{1,2},{2,3},{3,4},{4,5},{5,6},{6,7},{7,0},{8,9},{9,10},{10,1... | collective-permute-start | bytes 786440 | tf_op jit(solution)/shard_map/ppermute | solution.py:14
  94.2 122.6 %collective-permute-start.6 = (f32[2,128,256]{2,1,0:T(8,128)}, f32[2,128,256]{2,1,0:T(8,128)S(1)}, u32[]{:S(2)}, u32[]{:S(2)}) collective-permute-start(f32[2,128,256]{2,1,0:T(8,128)} %get-tuple-element.32), channel_id=1, source_target_pairs={{0,7},{1,0},{2,1},{3,2},{4,3},{5,4},{6,5},{7,6},{8,15},{9,8},{10,9... | collective-permute-start | bytes 786440 | tf_op jit(solution)/shard_map/ppermute | solution.py:14
  213.0 352.8 %collective-permute-start.5 = (f32[2,128,256]{2,1,0:T(8,128)}, f32[2,128,256]{2,1,0:T(8,128)}, u32[]{:S(2)}, u32[]{:S(2)}) collective-permute-start(f32[2,128,256]{2,1,0:T(8,128)} %collective-permute-done.4), channel_id=1, source_target_pairs={{0,8},{8,16},{16,24},{24,32},{32,40},{40,48},{48,56},{56,64},{64,7... | collective-permute-start | bytes 786440 | tf_op jit(solution)/shard_map/ppermute | solution.py:20
  216.8 350.7 %collective-permute-start.7 = (f32[2,128,256]{2,1,0:T(8,128)S(1)}, f32[2,128,256]{2,1,0:T(8,128)}, u32[]{:S(2)}, u32[]{:S(2)}) collective-permute-start(f32[2,128,256]{2,1,0:T(8,128)S(1)} %collective-permute-done.6), channel_id=1, source_target_pairs={{8,0},{16,8},{24,16},{32,24},{40,32},{48,40},{56,48},{64,56},{72,6... | collective-permute-start | bytes 786440 | tf_op jit(solution)/shard_map/ppermute | solution.py:20
Sparse Core Ops, SparseCore 0:
  102.3 461.7 all-reduce.1
where the time goes:
time: 580 us; the launch traced here: 578 us
  waiting for transfers between devices  351 us (61%)
  blocking collectives  111 us (19%)
  starting transfers between devices  60.4 us (10%)
  other arithmetic  18.4 us (3%)
  between operations  14.3 us (2%)
  local copies, waits for them, and re-layouts  13.2 us (2%)
  matrix products  10.2 us (2%)
    psum x1, waiting for transfers between devices, on_device(): lax.psum((partial_weight, partial_bias), ('rows', 'cols'))  344 us
    psum x1, blocking collectives, on_device(): lax.psum((partial_weight, partial_bias), ('rows', 'cols'))  111 us
    ppermute x4, starting transfers between devices, shifted(): return lax.ppermute(value, axis, pairs)  36.7 us
    ppermute x4, starting transfers between devices, from_behind(): lax.ppermute(value, axis, [(source, source + steps) for source in range(i...  23.6 us
  transfers between devices with their start and end apart: 9, of which 3 were waited for; matrix products, arithmetic and copies ran while one was open for 2% of the time, Pallas kernels for 0%

commit v1 on v0

v1 whole, which is shorter than its diff:
```python
import math

import jax
import jax.numpy as jnp
from jax import lax
from jax.experimental import pallas as pl
from jax.experimental.pallas import tpu as pltpu
from jax.sharding import PartitionSpec as P

MESH = pl.DeviceIdType.MESH
F32 = jnp.float32
BF16 = jnp.bfloat16
BLK = 128
PAIR = 256
PAIRS = 6
SLOTS = 3
PLANE = 16
PIECE = 16


def dot(a, b):
    return jnp.dot(a, b, preferred_element_type=F32)


def dot_t(a, b):
    return lax.dot_general(a, b, (((0,), (0,)), ((), ())), preferred_element_type=F32)


def place():
    rows, cols = lax.axis_index("rows"), lax.axis_index("cols")
    return rows // 16, cols // 2, (cols % 2) * 8 + (rows // 2) % 8, rows % 2


def device(x, y, z, core):
    return ((x * 8 + z % 8) * 2 + core, y * 2 + z // 8)


def along(step):
    flat = (lax.axis_index("rows") * 8 + lax.axis_index("cols") + step + 512) % 512
    return (flat // 8, flat % 8)


def kernel(
    norm_scale,
    feat_hbm, adj_hbm, off_ref, cnt_ref, w_ref, bias_ref, cot_hbm,
    act_hbm, gf_hbm, gw_ref, gb_ref,
    x_ref, a_ref, cot_ref, tile_ref, edge_acc, u_ref, act_ref, gf_ref, gf_acc, gf_edge,
    halo, spill, landed, grad_half, bias_acc,
    from_core, plane_out, plane_in, z_near, z_far, full_half, other_half,
    load_sem, save_sem, halo_send, halo_recv, spill_send, spill_recv,
    core_send, core_recv, plane_send, plane_recv, near_send, near_recv, far_send, far_recv,
    gather_send, gather_recv, back_send, back_recv,
):
    x, y, z, core = place()
    mine = x * 4 + y
    group, member = z // 4, z % 4

    def plane_peer(step):
        j = (mine + step) % PLANE
        return j, device(j // 4, j % 4, z, core)

    def near_peer(step):
        m = (member + step) % 4
        return device(x, y, group * 4 + m, core)

    def far_peer(step):
        g = (group + step) % 4
        return device(x, y, g * 4 + member, core)

    other_core = device(x, y, z, 1 - core)

    entry = pltpu.get_barrier_semaphore()

    def greet(target):
        pl.semaphore_signal(entry, inc=1, device_id=target, device_id_type=MESH)

    greet(along(1))
    greet(along(-1))
    for step in range(1, 4):
        greet(far_peer(step))
    for step in range(1, PLANE):
        greet(plane_peer(step)[1])
    for step in range(1, 4):
        greet(near_peer(step))
    greet(other_core)

    loads = [
        pltpu.make_async_copy(adj_hbm, a_ref.at[pl.ds(0, 2 * PAIRS)], load_sem.at[0]),
        pltpu.make_async_copy(feat_hbm, x_ref, load_sem.at[1]),
        pltpu.make_async_copy(cot_hbm, cot_ref, load_sem.at[2]),
    ]
    for load in loads:
        load.start()
    for s in range(SLOTS):
        a_ref[2 * PAIRS, s] = jnp.zeros((BLK, BLK), BF16)
    bias_acc[...] = jnp.zeros_like(bias_acc)
    grad_half[...] = jnp.zeros_like(grad_half)
    loads[0].wait()

    def build(p, carry):
        for r in range(2):
            i = 2 * p + r
            count = cnt_ref[i]
            offs = [off_ref[i, s] for s in range(SLOTS)]
            for q in range(3):
                for c in range(2):
                    k = 2 * (q - 1) + c - r
                    at = (pl.ds(r * BLK, BLK), pl.ds(c * BLK, BLK))
                    if abs(k) > 2:
                        tile_ref[p, q, at[0], at[1]] = jnp.zeros((BLK, BLK), BF16)
                        continue
                    row, slot = jnp.int32(2 * PAIRS), jnp.int32(0)
                    for s in range(SLOTS):
                        hit = jnp.logical_and(offs[s] == k, s < count)
                        row = jnp.where(hit, i, row)
                        slot = jnp.where(hit, s, slot)
                    tile_ref[p, q, at[0], at[1]] = a_ref[row, slot]
        return carry

    lax.fori_loop(0, PAIRS, build, 0)
    loads[1].wait()
    loads[2].wait()

    def layer(p, summed):
        rows = pl.ds(pl.multiple_of(p * PAIR, PAIR), PAIR)
        agg = summed.astype(BF16)
        pre = dot(agg, w_ref[...]) + bias_ref[...]
        q = jax.nn.sigmoid(pre)
        act_ref[rows, :] = (pre * q).astype(BF16)
        grad_pre = (cot_ref[rows, :].astype(F32) * q * (1.0 + pre * (1.0 - q))).astype(BF16)
        up = lax.dot_general(
            grad_pre, w_ref[...], (((1,), (1,)), ((), ())), preferred_element_type=F32
        ).astype(BF16)
        u_ref[p] = up
        gw = dot_t(agg, grad_pre)
        grad_half[0, pl.ds(0, PAIR)] += gw[:, :BLK]
        grad_half[1, pl.ds(0, PAIR)] += gw[:, BLK:]
        bias_acc[...] += jnp.sum(grad_pre.astype(F32).reshape(PAIR // 8, 8, PAIR), axis=0)

    def x_pair(p):
        return x_ref[pl.ds(pl.multiple_of(p * PAIR, PAIR), PAIR), :]

    def forward(p, carry):
        layer(
            p,
            dot(tile_ref[p, 0], x_pair(p - 1))
            + dot(tile_ref[p, 1], x_pair(p))
            + dot(tile_ref[p, 2], x_pair(p + 1)),
        )
        return carry

    lax.fori_loop(1, PAIRS - 1, forward, 0)

    pl.semaphore_wait(entry, 2 + 3 + 15 + 3 + 1)

    def rim(side):
        return pltpu.make_async_remote_copy(
            src_ref=x_ref.at[pl.ds((1 - side) * (PAIRS - 1) * PAIR, PAIR)],
            dst_ref=halo.at[side],
            send_sem=halo_send.at[side],
            recv_sem=halo_recv.at[side],
            device_id=along(1 - 2 * side),
            device_id_type=MESH,
        )

    rim(0).start()
    rim(1).start()

    def edge_start(side, carry):
        p = side * (PAIRS - 1)
        edge_acc[side] = dot(tile_ref[p, 1], x_pair(p)) + dot(
            tile_ref[p, 2 - 2 * side], x_pair(1 + 3 * side)
        )
        return carry

    lax.fori_loop(0, 2, edge_start, 0)

    def inner(side, carry):
        near = 1 + 3 * side
        deep = 2 + side
        gf_acc[side] = dot_t(tile_ref[near, 1], u_ref[near]) + dot_t(
            tile_ref[deep, 2 * side], u_ref[deep]
        )
        gf_edge[side] = dot_t(tile_ref[near, 2 * side], u_ref[near])
        total = (
            dot_t(tile_ref[deep - 1, 2], u_ref[deep - 1])
            + dot_t(tile_ref[deep, 1], u_ref[deep])
            + dot_t(tile_ref[deep + 1, 0], u_ref[deep + 1])
        )
        gf_ref[pl.ds(pl.multiple_of(deep * PAIR, PAIR), PAIR), :] = total.astype(BF16)
        return carry

    lax.fori_loop(0, 2, inner, 0)

    def back_copy(side):
        return pltpu.make_async_remote_copy(
            src_ref=spill.at[side],
            dst_ref=landed.at[1 - side],
            send_sem=spill_send.at[side],
            recv_sem=spill_recv.at[1 - side],
            device_id=along(2 * side - 1),
            device_id_type=MESH,
        )

    def edge(side, carry):
        p = side * (PAIRS - 1)
        rim(side).wait_recv()
        layer(p, edge_acc[side] + dot(tile_ref[p, 2 * side], halo[side]))
        up = u_ref[p]
        spill[side] = dot_t(tile_ref[p, 2 * side], up).astype(BF16)
        back_copy(side).start()
        near = 1 + 3 * side
        gf_ref[pl.ds(pl.multiple_of(near * PAIR, PAIR), PAIR), :] = (
            gf_acc[side] + dot_t(tile_ref[p, 2 - 2 * side], up)
        ).astype(BF16)
        gf_edge[side] += dot_t(tile_ref[p, 1], up)
        return carry

    lax.fori_loop(0, 2, edge, 0)

    grad_half[0, pl.ds(PAIR, 8)] = bias_acc[:, :BLK]
    grad_half[1, pl.ds(PAIR, 8)] = bias_acc[:, BLK:]
    to_core = pltpu.make_async_remote_copy(
        src_ref=grad_half.at[1 - core], dst_ref=from_core, send_sem=core_send, recv_sem=core_recv,
        device_id=other_core, device_id_type=MESH,
    )
    to_core.start()
    inner_rows = pl.ds(PAIR, (PAIRS - 2) * PAIR)
    saves = [
        pltpu.make_async_copy(act_ref, act_hbm, save_sem.at[0]),
        pltpu.make_async_copy(gf_ref.at[inner_rows], gf_hbm.at[inner_rows], save_sem.at[1]),
    ]
    for save in saves:
        save.start()
    to_core.wait()
    bias_rows = grad_half[core, pl.ds(PAIR, 8)] + from_core[pl.ds(PAIR, 8)]
    for j in range(PLANE):
        rows = pl.ds(j * PIECE, PIECE)
        plane_out[j, pl.ds(0, PIECE)] = grad_half[core, rows] + from_core[rows]
        plane_out[j, pl.ds(PIECE, 8)] = bias_rows

    def plane_copy(step):
        j, target = plane_peer(step)
        return pltpu.make_async_remote_copy(
            src_ref=plane_out.at[j], dst_ref=plane_in.at[mine],
            send_sem=plane_send.at[j], recv_sem=plane_recv.at[mine],
            device_id=target, device_id_type=MESH,
        )

    def plane_arrival(step):
        j, target = plane_peer(step)
        return pltpu.make_async_remote_copy(
            src_ref=plane_out.at[j], dst_ref=plane_in.at[j],
            send_sem=plane_send.at[j], recv_sem=plane_recv.at[j],
            device_id=target, device_id_type=MESH,
        )

    for step in range(1, PLANE):
        plane_copy(step).start()
    plane_in[mine] = plane_out[mine]
    for step in range(1, PLANE):
        plane_arrival(step).wait()
    total = plane_in[0]
    for j in range(1, PLANE):
        total = total + plane_in[j]

    z_near[member] = total

    def near_copy(step):
        return pltpu.make_async_remote_copy(
            src_ref=z_near.at[member], dst_ref=z_near.at[member],
            send_sem=near_send.at[step - 1], recv_sem=near_recv.at[member],
            device_id=near_peer(step), device_id_type=MESH,
        )

    def near_arrival(step):
        m = (member + step) % 4
        return pltpu.make_async_remote_copy(
            src_ref=z_near.at[m], dst_ref=z_near.at[m],
            send_sem=near_send.at[step - 1], recv_sem=near_recv.at[m],
            device_id=near_peer(step), device_id_type=MESH,
        )

    for step in range(1, 4):
        near_copy(step).start()
    for step in range(1, 4):
        near_arrival(step).wait()
    z_far[group] = (z_near[0] + z_near[1]) + (z_near[2] + z_near[3])

    def far_copy(step):
        return pltpu.make_async_remote_copy(
            src_ref=z_far.at[group], dst_ref=z_far.at[group],
            send_sem=far_send.at[step - 1], recv_sem=far_recv.at[group],
            device_id=far_peer(step), device_id_type=MESH,
        )

    def far_arrival(step):
        g = (group + step) % 4
        return pltpu.make_async_remote_copy(
            src_ref=z_far.at[g], dst_ref=z_far.at[g],
            send_sem=far_send.at[step - 1], recv_sem=far_recv.at[g],
            device_id=far_peer(step), device_id_type=MESH,
        )

    for step in range(1, 4):
        far_copy(step).start()

    def finish(side):
        back_copy(1 - side).wait_recv()
        rows = pl.ds(side * (PAIRS - 1) * PAIR, PAIR)
        gf_ref[rows, :] = (gf_edge[side] + landed[side].astype(F32)).astype(BF16)
        save = pltpu.make_async_copy(gf_ref.at[rows], gf_hbm.at[rows], save_sem.at[2 + side])
        save.start()
        return save

    for step in range(1, 4):
        far_arrival(step).wait()
    total = ((z_far[0] + z_far[1]) + (z_far[2] + z_far[3])) * norm_scale
    full_half[pl.ds(pl.multiple_of(mine * PIECE, PIECE), PIECE), :] = total[:PIECE]
    full_half[pl.ds(PAIR, 8), :] = jnp.broadcast_to(jnp.sum(total[PIECE:], axis=0, keepdims=True), (8, BLK))

    def piece(j):
        return full_half.at[pl.ds(pl.multiple_of(j * PIECE, PIECE), PIECE)]

    def gather_copy(step):
        j, target = plane_peer(step)
        return pltpu.make_async_remote_copy(
            src_ref=piece(mine), dst_ref=piece(mine),
            send_sem=gather_send.at[j], recv_sem=gather_recv.at[mine],
            device_id=target, device_id_type=MESH,
        )

    def gather_arrival(step):
        j, target = plane_peer(step)
        return pltpu.make_async_remote_copy(
            src_ref=piece(j), dst_ref=piece(j),
            send_sem=gather_send.at[j], recv_sem=gather_recv.at[j],
            device_id=target, device_id_type=MESH,
        )

    for step in range(1, PLANE):
        gather_copy(step).start()
    saves.append(finish(1))
    for step in range(1, PLANE):
        gather_arrival(step).wait()
    across = pltpu.make_async_remote_copy(
        src_ref=full_half, dst_ref=other_half, send_sem=back_send, recv_sem=back_recv,
        device_id=other_core, device_id_type=MESH,
    )
    across.start()
    across.wait()
    low = jnp.where(core == 0, full_half[...], other_half[...])
    high = jnp.where(core == 0, other_half[...], full_half[...])
    gw_ref[:, :BLK] = low[:PAIR]
    gw_ref[:, BLK:] = high[:PAIR]
    gb_ref[:, :BLK] = low[PAIR : PAIR + 1]
    gb_ref[:, BLK:] = high[PAIR : PAIR + 1]
    saves.append(finish(0))
    for side in range(2):
        rim(side).wait_send()
        back_copy(side).wait_send()
    for save in saves:
        save.wait()


def on_device(features, adj_values, adj_offset, adj_count, weight, bias_vector, cotangent):
    import functools

    nodes, width = features.shape
    nodes_total = nodes * lax.axis_size("rows") * lax.axis_size("cols")
    vmem = pl.BlockSpec(memory_space=pltpu.VMEM)
    smem = pl.BlockSpec(memory_space=pltpu.SMEM)
    anywhere = pl.BlockSpec(memory_space=pl.ANY)
    sem = pltpu.SemaphoreType.DMA
    activated, grad_features, grad_weight, grad_bias = pl.pallas_call(
        functools.partial(kernel, 1.0 / math.sqrt(nodes_total)),
        out_shape=(
            jax.ShapeDtypeStruct((nodes, width), BF16),
            jax.ShapeDtypeStruct((nodes, width), BF16),
            jax.ShapeDtypeStruct((width, width), F32),
            jax.ShapeDtypeStruct((1, width), F32),
        ),
        in_specs=[anywhere, anywhere, smem, smem, vmem, vmem, anywhere],
        out_specs=(anywhere, anywhere, vmem, vmem),
        scratch_shapes=[
            pltpu.VMEM((nodes, width), BF16),
            pltpu.VMEM((2 * PAIRS + 1, SLOTS, BLK, BLK), BF16),
            pltpu.VMEM((nodes, width), BF16),
            pltpu.VMEM((PAIRS, 3, PAIR, PAIR), BF16),
            pltpu.VMEM((2, PAIR, width), F32),
            pltpu.VMEM((PAIRS, PAIR, width), BF16),
            pltpu.VMEM((nodes, width), BF16),
            pltpu.VMEM((nodes, width), BF16),
            pltpu.VMEM((2, PAIR, width), F32),
            pltpu.VMEM((2, PAIR, width), F32),
            pltpu.VMEM((2, PAIR, width), BF16),
            pltpu.VMEM((2, PAIR, width), BF16),
            pltpu.VMEM((2, PAIR, width), BF16),
            pltpu.VMEM((2, PAIR + 8, BLK), F32),
            pltpu.VMEM((8, width), F32),
            pltpu.VMEM((PAIR + 8, BLK), F32),
            pltpu.VMEM((PLANE, PIECE + 8, BLK), F32),
            pltpu.VMEM((PLANE, PIECE + 8, BLK), F32),
            pltpu.VMEM((4, PIECE + 8, BLK), F32),
            pltpu.VMEM((4, PIECE + 8, BLK), F32),
            pltpu.VMEM((PAIR + 8, BLK), F32),
            pltpu.VMEM((PAIR + 8, BLK), F32),
            sem((3,)), sem((4,)), sem((2,)), sem((2,)), sem((2,)), sem((2,)),
            sem, sem, sem((PLANE,)), sem((PLANE,)), sem((3,)), sem((4,)), sem((3,)), sem((4,)),
            sem((PLANE,)), sem((PLANE,)), sem, sem,
        ],
        compiler_params=pltpu.CompilerParams(
            collective_id=0, has_side_effects=True, vmem_limit_bytes=56 << 20
        ),
        name="graph_layer",
    )(features, adj_values, adj_offset, adj_count, weight, bias_vector.reshape(1, width), cotangent)
    return activated, grad_features, grad_weight, grad_bias.reshape(width)


def solution(mesh):
    both = ("rows", "cols")
    return jax.shard_map(
        on_device,
        mesh=mesh,
        in_specs=(P(both, None), P(both, None, None, None), P(both, None), P(both), P(), P(), P(both, None)),
        out_specs=(P(both, None), P(both, None), P(), P()),
        check_vma=False,
    )
```

time: 580 us -> 104 us (0.18)
  waiting for transfers between devices: 351 us -> 0 us
  blocking collectives: 111 us -> 0 us
  Pallas kernels: 0 us -> 97.5 us
  starting transfers between devices: 60.4 us -> 0 us
  other arithmetic: 18.4 us -> 0 us
  between operations: 14.3 us -> 0.66 us
  matrix products: 10.2 us -> 0 us
  local copies, waits for them, and re-layouts: 13.2 us -> 5.67 us
    psum x1 -> x0, waiting for transfers between devices: 344 us -> none  [on_device(): lax.psum((partial_weight, partial_bias), ('rows', 'cols'))]
    psum x1 -> x0, blocking collectives: 111 us -> none  [on_device(): lax.psum((partial_weight, partial_bias), ('rows', 'cols'))]
    pallas_call x0 -> x1, Pallas kernels: none -> 97.5 us  [on_device(): pl.pallas_call(functools.partial(kernel, 1.0 / math.sqrt(nodes_total)), o...]
    ppermute x8 -> x0, starting transfers between devices: 60.3 us -> none  [the longest x4 36.7 us: shifted(): return lax.ppermute(value, axis, pairs)]
    scatter-add x3 -> x0, other arithmetic: 12.3 us -> none  [the longest x1 8.84 us: on_device(): empty.at[target.reshape(-1)]]
    dot_general x5 -> x0, matrix products: 10.2 us -> none  [the longest x1 3.07 us: on_device(): jnp.einsum('bsac,baf->bscf', adj_values, upstream.reshape(blocks, block_r...]
    ppermute x8 -> x0, waiting for transfers between devices: 6.95 us -> none  [the longest x4 6.01 us: shifted(): return lax.ppermute(value, axis, pairs)]
    reshape x2 -> x0, local copies, waits for them, and re-layouts: 6.23 us -> none  [the longest x1 6.15 us: on_device(): slot_terms.reshape(-1, block_rows, feat_width)]
  transfers between devices with their start and end apart: 9 -> 0, of which waited for: 3 -> 0; matrix products, arithmetic and copies ran while one was open for 2% -> 0% of each run, Pallas kernels for 0% -> 0%
where the time goes in v1:
time: 104 us
  Pallas kernels  97.5 us (94%)
  local copies, waits for them, and re-layouts  5.67 us (5%)
    pallas_call x1, Pallas kernels, on_device(): pl.pallas_call(functools.partial(kernel, 1.0 / math.sqrt(nodes_total)), o...  97.5 us
    unnamed x11, local copies, waits for them, and re-layouts  5.67 us

profile of v1, /device:TPU:1, one launch (start us, length us, event | category | flops | bytes accessed | tf_op | source)
XLA Modules:
  0.0 103.8 jit_solution(15452198691138934758)
XLA Ops:
  0.6 1.4 %copy.11.off_ref = s32[12,3]{1,0:T(8,128)} copy(s32[12,3]{0,1:T(4,128)} %param.9) | data formatting | bytes 288 | tf_op args[2]
  2.0 97.5 %graph_layer.1 = (bf16[1536,256]{1,0:T(8,128)(2,1)}, bf16[1536,256]{1,0:T(8,128)(2,1)}, f32[256,256]{1,0:T(8,128)}, f32[1,256]{1,0:T(1,128)}) custom-call(bf16[1536,256]{1,0:T(8,128)(2,1)} %feat_hbm.1, bf16[12,3,128,128]{3,2,1,0:T(8,128)(2,1)} %adj_hbm.1, s32[12,3]{1,0:T(8,128)} %copy.11.off_ref, s32[12]{0:T(128)} %cnt_ref.1, bf16[256,256]{1,0:T(8,128)(2,1)} %w_ref.1, ...), custom_call_target="tpu_custom_call" | custom-call | tf_op jit(solution)/shard_map/graph_layer/pallas_call | solution.py:375
  99.5 0.0 copy-start
  99.5 0.0 copy-start.1
  99.5 2.1 %copy.16 = bf16[1536,256]{1,0:T(8,128)(2,1)} copy(bf16[1536,256]{1,0:T(8,128)(2,1)} %get-tuple-element.16) | data formatting | bytes 1572864
  101.6 0.0 copy-done
  101.6 0.0 copy-start.2
  101.6 0.9 copy.17
  102.5 0.0 copy-done.1
  102.5 0.7 copy.18
  103.2 0.0 copy-done.2
  103.2 0.6 copy.19
Async XLA Ops:
  99.5 2.2 %copy-start = (bf16[1536,256]{1,0:T(8,128)(2,1)S(1)}, bf16[1536,256]{1,0:T(8,128)(2,1)}, u32[]{:S(2)}) copy-start(bf16[1536,256]{1,0:T(8,128)(2,1)} %get-tuple-element.17) | copy-start | bytes 2359300
  99.5 3.0 %copy-start.1 = (f32[256,256]{1,0:T(8,128)S(1)}, f32[256,256]{1,0:T(8,128)}, u32[]{:S(2)}) copy-start(f32[256,256]{1,0:T(8,128)} %get-tuple-element.18) | copy-start | bytes 786436
  101.6 1.6 %copy-start.2 = (f32[1,256]{1,0:T(1,128)S(1)}, f32[1,256]{1,0:T(1,128)}, u32[]{:S(2)}) copy-start(f32[1,256]{1,0:T(1,128)} %get-tuple-element.11) | copy-start | bytes 3076

commit v2 on v1

--- a/solution.py
+++ b/solution.py
@@ -1,3 +1,4 @@
+import functools
 import math
 
 import jax
@@ -15,6 +16,7 @@
 PAIRS = 6
 SLOTS = 3
 PLANE = 16
+PARTS = 4
 PIECE = 16
 
 
@@ -43,11 +45,11 @@
 def kernel(
     norm_scale,
     feat_hbm, adj_hbm, off_ref, cnt_ref, w_ref, bias_ref, cot_hbm,
-    act_hbm, gf_hbm, gw_ref, gb_ref,
-    x_ref, a_ref, cot_ref, tile_ref, edge_acc, u_ref, act_ref, gf_ref, gf_acc, gf_edge,
+    act_ref, gf_ref, gw_ref, gb_ref,
+    x_ref, a_ref, cot_ref, tile_ref, edge_acc, u_ref, gf_acc, gf_edge,
     halo, spill, landed, grad_half, bias_acc,
     from_core, plane_out, plane_in, z_near, z_far, full_half, other_half,
-    load_sem, save_sem, halo_send, halo_recv, spill_send, spill_recv,
+    load_sem, halo_send, halo_recv, spill_send, spill_recv,
     core_send, core_recv, plane_send, plane_recv, near_send, near_recv, far_send, far_recv,
     gather_send, gather_recv, back_send, back_recv,
 ):
@@ -101,7 +103,7 @@
         for r in range(2):
             i = 2 * p + r
             count = cnt_ref[i]
-            offs = [off_ref[i, s] for s in range(SLOTS)]
+            offs = [off_ref[s, i] for s in range(SLOTS)]
             for q in range(3):
                 for c in range(2):
                     k = 2 * (q - 1) + c - r
@@ -164,7 +166,6 @@
         )
 
     rim(0).start()
-    rim(1).start()
 
     def edge_start(side, carry):
         p = side * (PAIRS - 1)
@@ -191,32 +192,41 @@
         return carry
 
     lax.fori_loop(0, 2, inner, 0)
-
-    def back_copy(side):
-        return pltpu.make_async_remote_copy(
-            src_ref=spill.at[side],
-            dst_ref=landed.at[1 - side],
-            send_sem=spill_send.at[side],
-            recv_sem=spill_recv.at[1 - side],
+    rim(0).wait_send()
+    rim(1).start()
+
+    def back_copy(side, part):
+        rows = pl.ds(part * (PAIR // PARTS), PAIR // PARTS)
+        return pltpu.make_async_remote_copy(
+            src_ref=spill.at[side, rows],
+            dst_ref=landed.at[1 - side, rows],
+            send_sem=spill_send.at[side, part],
+            recv_sem=spill_recv.at[1 - side, part],
             device_id=along(2 * side - 1),
             device_id_type=MESH,
         )
 
-    def edge(side, carry):
+    def edge_layer(side):
         p = side * (PAIRS - 1)
         rim(side).wait_recv()
         layer(p, edge_acc[side] + dot(tile_ref[p, 2 * side], halo[side]))
+
+    def edge_back(side):
+        p = side * (PAIRS - 1)
         up = u_ref[p]
         spill[side] = dot_t(tile_ref[p, 2 * side], up).astype(BF16)
-        back_copy(side).start()
+        if side == 0:
+            for part in range(PARTS):
+                back_copy(0, part).start()
         near = 1 + 3 * side
-        gf_ref[pl.ds(pl.multiple_of(near * PAIR, PAIR), PAIR), :] = (
+        gf_ref[pl.ds(near * PAIR, PAIR), :] = (
             gf_acc[side] + dot_t(tile_ref[p, 2 - 2 * side], up)
         ).astype(BF16)
         gf_edge[side] += dot_t(tile_ref[p, 1], up)
-        return carry
-
-    lax.fori_loop(0, 2, edge, 0)
+
+    edge_layer(0)
+    edge_back(0)
+    edge_layer(1)
 
     grad_half[0, pl.ds(PAIR, 8)] = bias_acc[:, :BLK]
     grad_half[1, pl.ds(PAIR, 8)] = bias_acc[:, BLK:]
@@ -225,13 +235,8 @@
         device_id=other_core, device_id_type=MESH,
     )
     to_core.start()
-    inner_rows = pl.ds(PAIR, (PAIRS - 2) * PAIR)
-    saves = [
-        pltpu.make_async_copy(act_ref, act_hbm, save_sem.at[0]),
-        pltpu.make_async_copy(gf_ref.at[inner_rows], gf_hbm.at[inner_rows], save_sem.at[1]),
-    ]
-    for save in saves:
-        save.start()
+    edge_back(1)
+    back_copy(1, 0).start()
     to_core.wait()
     bias_rows = grad_half[core, pl.ds(PAIR, 8)] + from_core[pl.ds(PAIR, 8)]
     for j in range(PLANE):
@@ -283,6 +288,7 @@
 
     for step in range(1, 4):
         near_copy(step).start()
+    back_copy(1, 1).start()
     for step in range(1, 4):
         near_arrival(step).wait()
     z_far[group] = (z_near[0] + z_near[1]) + (z_near[2] + z_near[3])
@@ -304,14 +310,14 @@
 
     for step in range(1, 4):
         far_copy(step).start()
+    back_copy(1, 2).start()
+    back_copy(1, 3).start()
 
     def finish(side):
-        back_copy(1 - side).wait_recv()
+        for part in range(PARTS):
+            back_copy(1 - side, part).wait_recv()
         rows = pl.ds(side * (PAIRS - 1) * PAIR, PAIR)
         gf_ref[rows, :] = (gf_edge[side] + landed[side].astype(F32)).astype(BF16)
-        save = pltpu.make_async_copy(gf_ref.at[rows], gf_hbm.at[rows], save_sem.at[2 + side])
-        save.start()
-        return save
 
     for step in range(1, 4):
         far_arrival(step).wait()
@@ -340,7 +346,7 @@
 
     for step in range(1, PLANE):
         gather_copy(step).start()
-    saves.append(finish(1))
+    finish(1)
     for step in range(1, PLANE):
         gather_arrival(step).wait()
     across = pltpu.make_async_remote_copy(
@@ -355,33 +361,39 @@
     gw_ref[:, BLK:] = high[:PAIR]
     gb_ref[:, :BLK] = low[PAIR : PAIR + 1]
     gb_ref[:, BLK:] = high[PAIR : PAIR + 1]
-    saves.append(finish(0))
+    finish(0)
+    rim(1).wait_send()
     for side in range(2):
-        rim(side).wait_send()
-        back_copy(side).wait_send()
-    for save in saves:
-        save.wait()
+        for part in range(PARTS):
+            back_copy(side, part).wait_send()
+
+
+def write_out(*refs):
+    sems = refs[-1]
+    copies = [pltpu.make_async_copy(refs[k], refs[4 + k], sems.at[k]) for k in range(4)]
+    for copy in copies:
+        copy.start()
+    for copy in copies:
+        copy.wait()
 
 
 def on_device(features, adj_values, adj_offset, adj_count, weight, bias_vector, cotangent):
-    import functools
-
     nodes, width = features.shape
     nodes_total = nodes * lax.axis_size("rows") * lax.axis_size("cols")
     vmem = pl.BlockSpec(memory_space=pltpu.VMEM)
     smem = pl.BlockSpec(memory_space=pltpu.SMEM)
     anywhere = pl.BlockSpec(memory_space=pl.ANY)
     sem = pltpu.SemaphoreType.DMA
-    activated, grad_features, grad_weight, grad_bias = pl.pallas_call(
+    results = pl.pallas_call(
         functools.partial(kernel, 1.0 / math.sqrt(nodes_total)),
         out_shape=(
-            jax.ShapeDtypeStruct((nodes, width), BF16),
-            jax.ShapeDtypeStruct((nodes, width), BF16),
-            jax.ShapeDtypeStruct((width, width), F32),
-            jax.ShapeDtypeStruct((1, width), F32),
+            pltpu.VMEM((nodes, width), BF16),
+            pltpu.VMEM((nodes, width), BF16),
+            pltpu.VMEM((width, width), F32),
+            pltpu.VMEM((1, width), F32),
         ),
         in_specs=[anywhere, anywhere, smem, smem, vmem, vmem, anywhere],
-        out_specs=(anywhere, anywhere, vmem, vmem),
+        out_specs=(vmem, vmem, vmem, vmem),
         scratch_shapes=[
             pltpu.VMEM((nodes, width), BF16),
             pltpu.VMEM((2 * PAIRS + 1, SLOTS, BLK, BLK), BF16),
@@ -389,8 +401,6 @@
             pltpu.VMEM((PAIRS, 3, PAIR, PAIR), BF16),
             pltpu.VMEM((2, PAIR, width), F32),
             pltpu.VMEM((PAIRS, PAIR, width), BF16),
-            pltpu.VMEM((nodes, width), BF16),
-            pltpu.VMEM((nodes, width), BF16),
             pltpu.VMEM((2, PAIR, width), F32),
             pltpu.VMEM((2, PAIR, width), F32),
             pltpu.VMEM((2, PAIR, width), BF16),
@@ -405,7 +415,7 @@
             pltpu.VMEM((4, PIECE + 8, BLK), F32),
             pltpu.VMEM((PAIR + 8, BLK), F32),
             pltpu.VMEM((PAIR + 8, BLK), F32),
-            sem((3,)), sem((4,)), sem((2,)), sem((2,)), sem((2,)), sem((2,)),
+            sem((3,)), sem((2,)), sem((2,)), sem((2, PARTS)), sem((2, PARTS)),
             sem, sem, sem((PLANE,)), sem((PLANE,)), sem((3,)), sem((4,)), sem((3,)), sem((4,)),
             sem((PLANE,)), sem((PLANE,)), sem, sem,
         ],
@@ -413,7 +423,20 @@
             collective_id=0, has_side_effects=True, vmem_limit_bytes=56 << 20
         ),
         name="graph_layer",
-    )(features, adj_values, adj_offset, adj_count, weight, bias_vector.reshape(1, width), cotangent)
+    )(features, adj_values, adj_offset.T, adj_count, weight, bias_vector.reshape(1, width), cotangent)
+    activated, grad_features, grad_weight, grad_bias = pl.pallas_call(
+        write_out,
+        out_shape=(
+            jax.ShapeDtypeStruct((nodes, width), BF16),
+            jax.ShapeDtypeStruct((nodes, width), BF16),
+            jax.ShapeDtypeStruct((width, width), F32),
+            jax.ShapeDtypeStruct((1, width), F32),
+        ),
+        in_specs=[vmem] * 4,
+        out_specs=(anywhere,) * 4,
+        scratch_shapes=[sem((4,))],
+        name="write_out",
+    )(*[pltpu.with_memory_space_constraint(r, pltpu.VMEM) for r in results])
     return activated, grad_features, grad_weight, grad_bias.reshape(width)
 
 

time: 104 us -> 94.9 us (0.913)
  the two profiles are of different devices: /device:TPU:1 before, /device:TPU:97 now
where the time goes in v2:
time: 94.9 us; the launch traced here: 94.8 us
  Pallas kernels  94.1 us (99%)
    pallas_call x1, Pallas kernels, on_device(): pl.pallas_call(functools.partial(kernel, 1.0 / math.sqrt(nodes_total)), o...  92.9 us

profile of v2, /device:TPU:97, one launch (start us, length us, event | category | flops | bytes accessed | tf_op | source)
XLA Modules:
  0.0 94.8 jit_solution(7308790731537618026)
XLA Ops:
  0.6 92.9 %graph_layer.1 = (bf16[1536,256]{1,0:T(8,128)(2,1)S(1)}, bf16[1536,256]{1,0:T(8,128)(2,1)S(1)}, f32[256,256]{1,0:T(8,128)S(1)}, f32[1,256]{1,0:T(1,128)S(1)}) custom-call(bf16[1536,256]{1,0:T(8,128)(2,1)} %feat_hbm.1, bf16[12,3,128,128]{3,2,1,0:T(8,128)(2,1)} %adj_hbm.1, s32[3,12]{1,0:T(4,128)} %bitcast.3, s32[12]{0:T(128)} %cnt_ref.1, ...), custom_call_target="tpu_custom_call" | custom-call | tf_op jit(solution)/shard_map/graph_layer/pallas_call | solution.py:387
  93.5 1.3 %write_out.1 = (bf16[1536,256]{1,0:T(8,128)(2,1)}, bf16[1536,256]{1,0:T(8,128)(2,1)}, f32[256,256]{1,0:T(8,128)}, f32[1,256]{1,0:T(1,128)}) custom-call(bf16[1536,256]{1,0:T(8,128)(2,1)S(1)} %get-tuple-element.12.refs_0_, bf16[1536,256]{1,0:T(8,128)(2,1)S(1)} %get-tuple-element.13.refs_1_, f32[256,256]{1,0:T(8,128)S(1)} %get-tuple-element.14.refs_2_, ...), custom_call_target="tpu_custom_call" | custom-call | tf_op jit(solution)/shard_map/write_out/pallas_call | solution.py:427

commit v3 on v2

--- a/solution.py
+++ b/solution.py
@@ -166,6 +166,7 @@
         )
 
     rim(0).start()
+    rim(1).start()
 
     def edge_start(side, carry):
         p = side * (PAIRS - 1)
@@ -192,8 +193,6 @@
         return carry
 
     lax.fori_loop(0, 2, inner, 0)
-    rim(0).wait_send()
-    rim(1).start()
 
     def back_copy(side, part):
         rows = pl.ds(part * (PAIR // PARTS), PAIR // PARTS)
@@ -215,9 +214,6 @@
         p = side * (PAIRS - 1)
         up = u_ref[p]
         spill[side] = dot_t(tile_ref[p, 2 * side], up).astype(BF16)
-        if side == 0:
-            for part in range(PARTS):
-                back_copy(0, part).start()
         near = 1 + 3 * side
         gf_ref[pl.ds(near * PAIR, PAIR), :] = (
             gf_acc[side] + dot_t(tile_ref[p, 2 - 2 * side], up)
@@ -236,6 +232,7 @@
     )
     to_core.start()
     edge_back(1)
+    back_copy(0, 0).start()
     back_copy(1, 0).start()
     to_core.wait()
     bias_rows = grad_half[core, pl.ds(PAIR, 8)] + from_core[pl.ds(PAIR, 8)]
@@ -288,6 +285,7 @@
 
     for step in range(1, 4):
         near_copy(step).start()
+    back_copy(0, 1).start()
     back_copy(1, 1).start()
     for step in range(1, 4):
         near_arrival(step).wait()
@@ -310,6 +308,8 @@
 
     for step in range(1, 4):
         far_copy(step).start()
+    back_copy(0, 2).start()
+    back_copy(0, 3).start()
     back_copy(1, 2).start()
     back_copy(1, 3).start()
 
@@ -362,6 +362,7 @@
     gb_ref[:, :BLK] = low[PAIR : PAIR + 1]
     gb_ref[:, BLK:] = high[PAIR : PAIR + 1]
     finish(0)
+    rim(0).wait_send()
     rim(1).wait_send()
     for side in range(2):
         for part in range(PARTS):

time: 94.9 us -> 86.9 us (0.916)
  the two profiles are of different devices: /device:TPU:97 before, /device:TPU:1 now
where the time goes in v3:
time: 86.9 us; the launch traced here: 86.5 us
  Pallas kernels  85.8 us (99%)
    pallas_call x1, Pallas kernels, on_device(): pl.pallas_call(functools.partial(kernel, 1.0 / math.sqrt(nodes_total)), o...  84.6 us

profile of v3, /device:TPU:1, one launch (start us, length us, event | category | flops | bytes accessed | tf_op | source)
XLA Modules:
  0.0 86.5 jit_solution(5849084521163630451)
XLA Ops:
  0.6 84.6 %graph_layer.1 = (bf16[1536,256]{1,0:T(8,128)(2,1)S(1)}, bf16[1536,256]{1,0:T(8,128)(2,1)S(1)}, f32[256,256]{1,0:T(8,128)S(1)}, f32[1,256]{1,0:T(1,128)S(1)}) custom-call(bf16[1536,256]{1,0:T(8,128)(2,1)} %feat_hbm.1, bf16[12,3,128,128]{3,2,1,0:T(8,128)(2,1)} %adj_hbm.1, s32[3,12]{1,0:T(4,128)} %bitcast.3, s32[12]{0:T(128)} %cnt_ref.1, ...), custom_call_target="tpu_custom_call" | custom-call | tf_op jit(solution)/shard_map/graph_layer/pallas_call | solution.py:388
  85.2 1.3 %write_out.1 = (bf16[1536,256]{1,0:T(8,128)(2,1)}, bf16[1536,256]{1,0:T(8,128)(2,1)}, f32[256,256]{1,0:T(8,128)}, f32[1,256]{1,0:T(1,128)}) custom-call(bf16[1536,256]{1,0:T(8,128)(2,1)S(1)} %get-tuple-element.12.refs_0_, bf16[1536,256]{1,0:T(8,128)(2,1)S(1)} %get-tuple-element.13.refs_1_, f32[256,256]{1,0:T(8,128)S(1)} %get-tuple-element.14.refs_2_, ...), custom_call_target="tpu_custom_call" | custom-call | tf_op jit(solution)/shard_map/write_out/pallas_call | solution.py:428

commit v4 on v3

--- a/solution.py
+++ b/solution.py
@@ -221,7 +221,6 @@
         gf_edge[side] += dot_t(tile_ref[p, 1], up)
 
     edge_layer(0)
-    edge_back(0)
     edge_layer(1)
 
     grad_half[0, pl.ds(PAIR, 8)] = bias_acc[:, :BLK]
@@ -231,9 +230,10 @@
         device_id=other_core, device_id_type=MESH,
     )
     to_core.start()
+    edge_back(0)
     edge_back(1)
+    back_copy(1, 0).start()
     back_copy(0, 0).start()
-    back_copy(1, 0).start()
     to_core.wait()
     bias_rows = grad_half[core, pl.ds(PAIR, 8)] + from_core[pl.ds(PAIR, 8)]
     for j in range(PLANE):
@@ -285,8 +285,8 @@
 
     for step in range(1, 4):
         near_copy(step).start()
+    back_copy(1, 1).start()
     back_copy(0, 1).start()
-    back_copy(1, 1).start()
     for step in range(1, 4):
         near_arrival(step).wait()
     z_far[group] = (z_near[0] + z_near[1]) + (z_near[2] + z_near[3])
@@ -308,10 +308,10 @@
 
     for step in range(1, 4):
         far_copy(step).start()
+    back_copy(1, 2).start()
     back_copy(0, 2).start()
+    back_copy(1, 3).start()
     back_copy(0, 3).start()
-    back_copy(1, 2).start()
-    back_copy(1, 3).start()
 
     def finish(side):
         for part in range(PARTS):
@@ -346,7 +346,6 @@
 
     for step in range(1, PLANE):
         gather_copy(step).start()
-    finish(1)
     for step in range(1, PLANE):
         gather_arrival(step).wait()
     across = pltpu.make_async_remote_copy(
@@ -361,6 +360,7 @@
     gw_ref[:, BLK:] = high[:PAIR]
     gb_ref[:, :BLK] = low[PAIR : PAIR + 1]
     gb_ref[:, BLK:] = high[PAIR : PAIR + 1]
+    finish(1)
     finish(0)
     rim(0).wait_send()
     rim(1).wait_send()

time: 86.9 us -> 86.8 us (level)
  no operation moved by 1% of the time
where the time goes in v4:
time: 86.8 us; the launch traced here: 86.6 us
  Pallas kernels  86 us (99%)
    pallas_call x1, Pallas kernels, on_device(): pl.pallas_call(functools.partial(kernel, 1.0 / math.sqrt(nodes_total)), o...  84.7 us

profile of v4, /device:TPU:1, one launch (start us, length us, event | category | flops | bytes accessed | tf_op | source)
XLA Modules:
  0.0 86.6 jit_solution(7227222521413368319)
XLA Ops:
  0.6 84.7 %graph_layer.1 = (bf16[1536,256]{1,0:T(8,128)(2,1)S(1)}, bf16[1536,256]{1,0:T(8,128)(2,1)S(1)}, f32[256,256]{1,0:T(8,128)S(1)}, f32[1,256]{1,0:T(1,128)S(1)}) custom-call(bf16[1536,256]{1,0:T(8,128)(2,1)} %feat_hbm.1, bf16[12,3,128,128]{3,2,1,0:T(8,128)(2,1)} %adj_hbm.1, s32[3,12]{1,0:T(4,128)} %bitcast.3, s32[12]{0:T(128)} %cnt_ref.1, ...), custom_call_target="tpu_custom_call" | custom-call | tf_op jit(solution)/shard_map/graph_layer/pallas_call | solution.py:388
  85.4 1.3 %write_out.1 = (bf16[1536,256]{1,0:T(8,128)(2,1)}, bf16[1536,256]{1,0:T(8,128)(2,1)}, f32[256,256]{1,0:T(8,128)}, f32[1,256]{1,0:T(1,128)}) custom-call(bf16[1536,256]{1,0:T(8,128)(2,1)S(1)} %get-tuple-element.12.refs_0_, bf16[1536,256]{1,0:T(8,128)(2,1)S(1)} %get-tuple-element.13.refs_1_, f32[256,256]{1,0:T(8,128)S(1)} %get-tuple-element.14.refs_2_, ...), custom_call_target="tpu_custom_call" | custom-call | tf_op jit(solution)/shard_map/write_out/pallas_call | solution.py:428

commit v5 on v3

--- a/solution.py
+++ b/solution.py
@@ -346,7 +346,6 @@
 
     for step in range(1, PLANE):
         gather_copy(step).start()
-    finish(1)
     for step in range(1, PLANE):
         gather_arrival(step).wait()
     across = pltpu.make_async_remote_copy(
@@ -361,6 +360,7 @@
     gw_ref[:, BLK:] = high[:PAIR]
     gb_ref[:, :BLK] = low[PAIR : PAIR + 1]
     gb_ref[:, BLK:] = high[PAIR : PAIR + 1]
+    finish(1)
     finish(0)
     rim(0).wait_send()
     rim(1).wait_send()

time: 86.9 us -> 86.9 us (level)
  no operation moved by 1% of the time
where the time goes in v5:
time: 86.9 us; the launch traced here: 86.5 us
  Pallas kernels  85.9 us (99%)
    pallas_call x1, Pallas kernels, on_device(): pl.pallas_call(functools.partial(kernel, 1.0 / math.sqrt(nodes_total)), o...  84.6 us

profile of v5, /device:TPU:1, one launch (start us, length us, event | category | flops | bytes accessed | tf_op | source)
XLA Modules:
  0.0 86.5 jit_solution(6593649606788701628)
XLA Ops:
  0.6 84.6 %graph_layer.1 = (bf16[1536,256]{1,0:T(8,128)(2,1)S(1)}, bf16[1536,256]{1,0:T(8,128)(2,1)S(1)}, f32[256,256]{1,0:T(8,128)S(1)}, f32[1,256]{1,0:T(1,128)S(1)}) custom-call(bf16[1536,256]{1,0:T(8,128)(2,1)} %feat_hbm.1, bf16[12,3,128,128]{3,2,1,0:T(8,128)(2,1)} %adj_hbm.1, s32[3,12]{1,0:T(4,128)} %bitcast.3, s32[12]{0:T(128)} %cnt_ref.1, ...), custom_call_target="tpu_custom_call" | custom-call | tf_op jit(solution)/shard_map/graph_layer/pallas_call | solution.py:388
  85.3 1.3 %write_out.1 = (bf16[1536,256]{1,0:T(8,128)(2,1)}, bf16[1536,256]{1,0:T(8,128)(2,1)}, f32[256,256]{1,0:T(8,128)}, f32[1,256]{1,0:T(1,128)}) custom-call(bf16[1536,256]{1,0:T(8,128)(2,1)S(1)} %get-tuple-element.12.refs_0_, bf16[1536,256]{1,0:T(8,128)(2,1)S(1)} %get-tuple-element.13.refs_1_, f32[256,256]{1,0:T(8,128)S(1)} %get-tuple-element.14.refs_2_, ...), custom_call_target="tpu_custom_call" | custom-call | tf_op jit(solution)/shard_map/write_out/pallas_call | solution.py:428
